TPU v7x, 256 devices: a whole 4x4x8 slice. The times are simulated.
256 devices in a mesh: dp: 32 (over x, y, z_lo), cent: 8 (over z_hi, core).
Axes of the slice: x: 4, y: 4, z: 8 (z_hi: 4, z_lo: 2; z = z_hi * 2 + z_lo), core: 2. Of those that a mesh axis runs over, the one named last changes fastest.
Arguments:
- points: bfloat16 [32768, 256], P('dp'), may hold values from -8 to 8
- centroids: bfloat16 [32768, 256], P('cent'), may hold values from -0.5 to 0.5
Outputs:
- new_centroids: float32 [32768, 256], P('cent')
- counts: float32 [32768], P('cent')
- log_evidence: float32 [32768], P('dp')
All inputs are finite; a program needn't handle non-finite values.
Results may differ from a plain program's by a relative error of at most 0.0016.
Values sent between devices are 32-bit elements; how exact they have to be, the bound alone decides.
A program may use at most 64 MiB of HBM per device.

v0:
```python
import math

import jax
import jax.numpy as jnp
from jax import lax
from jax.sharding import PartitionSpec as P

prior_mass = 0.5


def body(points, centroids):
    rows = points.shape[0]
    local_cent = centroids.shape[0]
    width = centroids.shape[1]
    every_centroid = local_cent * lax.axis_size("cent")
    block = min(512, rows)
    cnorm = jnp.einsum("kd,kd->k", centroids, centroids, preferred_element_type=jnp.float32)
    sums = jnp.zeros((local_cent, width), jnp.float32)
    counts = jnp.zeros((local_cent,), jnp.float32)
    evidence = []
    for step in range(rows // block):
        piece = lax.slice_in_dim(points, step * block, (step + 1) * block, axis=0)
        dots = jnp.einsum("nd,kd->nk", piece, centroids, preferred_element_type=jnp.float32)
        score = 2.0 * dots - cnorm[None, :]
        top = lax.pmax(jnp.max(score, axis=1), "cent")
        weights = jnp.exp(score - top[:, None])
        total = lax.psum(jnp.sum(weights, axis=1), "cent")
        resp = (weights / total[:, None]).astype(jnp.bfloat16)
        sums = sums + jnp.einsum("nk,nd->kd", resp, piece, preferred_element_type=jnp.float32)
        counts = counts + jnp.sum(resp.astype(jnp.float32), axis=0)
        evidence.append(top + jnp.log(total) - math.log(every_centroid))
    log_evidence = jnp.concatenate(evidence, axis=0)
    all_sums, all_counts = lax.psum((sums, counts), "dp")
    new_centroids = (all_sums + prior_mass * centroids.astype(jnp.float32)) / (
        all_counts + prior_mass
    )[:, None]
    return (new_centroids, all_counts, log_evidence)


def solution(mesh):
    return jax.shard_map(
        body,
        mesh=mesh,
        in_specs=(P("dp", None), P("cent", None)),
        out_specs=(P("cent", None), P("cent"), P("dp")),
        check_vma=False,
    )
```

profile of v0, /device:TPU:8, one launch (start us, length us, event | category | flops | bytes accessed | tf_op | source)
XLA Modules:
  0.0 421.0 jit_solution(17040239577599494853)
XLA Ops:
  7.2 0.0 copy-start.1
  7.2 0.0 copy-start.2
  7.2 0.0 all-reduce.4.cloned.1.call-start
  7.2 2.4 fusion.4
  9.6 3.0 fusion.12
  12.6 0.0 copy-done.1
  12.6 0.0 copy-done.2
  12.6 0.0 copy-start
  12.6 4.9 %fusion.1 = (f32[512]{0:T(512)S(1)}, f32[512]{0:T(512)S(1)}, f32[512,4096]{1,0:T(8,128)}) fusion(f32[4096]{0:T(1024)S(1)} %fusion.4, f32[512,4096]{1,0:T(8,128)S(1)} %fusion.12, bf16[4096,256]{1,0:T(8,128)(2,1)S(1)} %copy-done.1, bf16[1024,256]{1,0:T(8,128)(2,1)S(1)} %copy-done.2), kind=kOutput, calls=%fused_computation.9 | convolution fusion | flops 1086323712 | bytes 19156992 | tf_op jit(solution)/shard_map/nd,kd->nk/dot_general | solution.py:23
  17.6 0.8 copy-done
  18.3 19.9 %all-reduce.1 = (f32[512]{0:T(512)S(1)}, f32[512]{0:T(512)S(1)}) all-reduce(f32[512]{0:T(512)S(1)} %get-tuple-element.5, f32[512]{0:T(512)S(1)} %get-tuple-element.6), channel_id=1, replica_groups=mesh['dp'=32,'cent'=8] {'cent'}, use_global_device_ids=true, to_apply=%region_5.0 | all-reduce | flops 1024 | bytes 8192 | tf_op jit(solution)/shard_map/pmax | solution.py:25
  38.2 7.6 %fusion.3 = (f32[512]{0:T(512)S(1)}, f32[512]{0:T(512)S(1)}) fusion(f32[512,4096]{1,0:T(8,128)} %get-tuple-element.17, f32[512]{0:T(512)S(1)} %get-tuple-element.9, f32[4096]{0:T(1024)S(1)} %fusion.4, f32[512]{0:T(512)S(1)} %get-tuple-element.10, f32[512,4096]{1,0:T(8,128)} %copy-done), kind=kLoop, calls=%fused_computation.11 | loop fusion | flops 16776192 | bytes 16801792 | tf_op jit(solution)/shard_map/reduce_sum | solution.py:27
  45.9 14.2 %all-reduce = (f32[512]{0:T(512)S(1)}, f32[512]{0:T(512)S(1)}) all-reduce(f32[512]{0:T(512)S(1)} %get-tuple-element.4, f32[512]{0:T(512)S(1)} %get-tuple-element.3), channel_id=1, replica_groups=mesh['dp'=32,'cent'=8] {'cent'}, use_global_device_ids=true, to_apply=%region_3.0 | all-reduce | flops 1024 | bytes 8192 | tf_op jit(solution)/shard_map/psum | solution.py:27
  60.1 8.7 %convert_reduce_fusion = (f32[4096]{0:T(1024)S(1)}, bf16[512,4096]{1,0:T(8,128)(2,1)S(1)}, f32[4096]{0:T(1024)S(1)}, bf16[512,4096]{1,0:T(8,128)(2,1)S(1)}) fusion(f32[512]{0:T(512)S(1)} %get-tuple-element.8, f32[512]{0:T(512)S(1)} %get-tuple-element.9, f32[4096]{0:T(1024)S(1)} %fusion.4, f32[512,4096]{1,0:T(8,128)} %get-tuple-element.17, ...), kind=kLoop, calls=%fused_computation | loop fusion | flops 29351936 | bytes 25223168 | tf_op jit(solution)/shard_map/reduce_sum | solution.py:30
  68.8 1.3 fusion.10
  70.1 3.4 convolution_add_fusion
  73.5 0.0 all-reduce.4.cloned.1.call-update
  73.5 154.6 %psum.31 = f32[4096]{0:T(1024)S(1)} all-reduce(f32[4096]{0:T(1024)S(1)} %add.33), channel_id=1, replica_groups=mesh['dp'=32,'cent'=8] {'dp'}, use_global_device_ids=true, to_apply=%region_11.0 | all-reduce | flops 4096 | bytes 32768 | tf_op jit(solution)/shard_map/psum | solution.py:33
  228.1 0.0 copy-start.3
  228.1 0.6 pad_maximum_fusion
  228.7 181.6 %all-reduce.4.cloned.1.call-done = f32[4096,256]{1,0:T(8,128)} async-done(((f32[4096,256]{1,0:T(8,128)}), f32[4096,256]{1,0:T(8,128)}) %all-reduce.4.cloned.1.call-update) | async-done | bytes 4194320 | tf_op jit(solution)/shard_map/psum | solution.py:33
  410.2 3.9 fusion.6
  414.2 0.0 copy-done.3
  (3 shorter events, 0.0 us)
Async XLA Ops:
  7.2 5.4 %copy-start.1 = (bf16[4096,256]{1,0:T(8,128)(2,1)S(1)}, bf16[4096,256]{1,0:T(8,128)(2,1)}, u32[]{:S(2)}) copy-start(bf16[4096,256]{1,0:T(8,128)(2,1)} %param.3) | copy-start | bytes 6291460
  7.2 5.4 %copy-start.2 = (bf16[1024,256]{1,0:T(8,128)(2,1)S(1)}, bf16[1024,256]{1,0:T(8,128)(2,1)}, u32[]{:S(2)}) copy-start(bf16[1024,256]{1,0:T(8,128)(2,1)} %param.2) | copy-start | bytes 1572868
  7.2 403.0 %all-reduce.4.cloned.1.call-start = ((), (), s32[]{:S(2)}) async-start(), calls=%async_computation | async-start | bytes 8388608 | tf_op jit(solution)/shard_map/psum | solution.py:33
  12.6 5.7 %copy-start = (f32[512,4096]{1,0:T(8,128)}, f32[512,4096]{1,0:T(8,128)S(1)}, u32[]{:S(2)}) copy-start(f32[512,4096]{1,0:T(8,128)S(1)} %fusion.12) | copy-start | bytes 25165828
  228.1 186.1 %copy-start.3 = (f32[4096]{0:T(1024)}, f32[4096]{0:T(1024)S(1)}, u32[]{:S(2)}) copy-start(f32[4096]{0:T(1024)S(1)} %psum.31) | copy-start | bytes 49156
Sparse Core Ops, SparseCore 0:
  73.6 336.5 all-reduce.3
where the time goes:
time: 425 us; the launch traced here: 421 us
  blocking collectives  189 us (44%)
  waiting for transfers between devices  182 us (43%)
  other arithmetic  23.2 us (5%)
  between operations  14.1 us (3%)
  matrix products  12.6 us (3%)
    psum x1, waiting for transfers between devices, body(): all_sums, all_counts = lax.psum((sums, counts), 'dp')  182 us
    psum x1, blocking collectives, body(): all_sums, all_counts = lax.psum((sums, counts), 'dp')  155 us
    pmax x1, blocking collectives, body(): top = lax.pmax(jnp.max(score, axis=1), 'cent')  19.9 us
    psum x1, blocking collectives, body(): total = lax.psum(jnp.sum(weights, axis=1), 'cent')  14.2 us
    reduce_sum x1, other arithmetic, body(): counts = counts + jnp.sum(resp.astype(jnp.float32), axis=0)  8.66 us
  transfers between devices with their start and end apart: 1, of which 1 were waited for; matrix products, arithmetic and copies ran while one was open for 0% of the time, Pallas kernels for 0%

commit v1 on v0

v1 whole, which is shorter than its diff:
```python
import functools
import math

import jax
import jax.numpy as jnp
from jax import lax
from jax.experimental import pallas as pl
from jax.experimental.pallas import tpu as pltpu
from jax.sharding import PartitionSpec as P

MESH = pl.DeviceIdType.MESH
prior_mass = 0.5

NX, NY, NZ = 4, 4, 2
BLOCKS = 4
TILE = 256
F32, BF16 = jnp.float32, jnp.bfloat16

ORDER = None


def stage_order(blocks, stages):
    order = [(0, 0), (1, 0)]
    step = 2
    for tau in range(1, stages + step * blocks):
        for s in range(blocks):
            stage = tau - step * s
            if s >= 1:
                stage = tau - step * (s - 1) - 1
            if 0 <= stage < stages and (s, stage) not in order:
                order.append((s, stage))
    return order


def kernel(sizes, x_ref, c_ref, sum_ref, count_ref, log_ref,
           xt, xs, et, cb, part, rxu, rxv, rxz, soft, q, qr,
           soft_send, soft_recv, q_send, q_recv, send, recv):
    rows, cents, width, groups = sizes
    every_centroid = cents * groups
    dp, cent = lax.axis_index("dp"), lax.axis_index("cent")
    px, py, pz = dp // (NY * NZ), (dp // NZ) % NY, dp % NZ

    def at(x=None, y=None, z=None):
        x = px if x is None else x
        y = py if y is None else y
        z = pz if z is None else z
        return {"dp": (x * NY + y) * NZ + z, "cent": cent}

    def along(axis, offset):
        if axis == 0:
            return at(x=(px + offset) % NX)
        return at(y=(py + offset) % NY)

    partners = [along(a, d) for a in (0, 1) for d in (1, 2, 3)] + [at(z=1 - pz)]
    partners += [{"dp": dp, "cent": (cent + d) % groups} for d in range(1, groups)]
    barrier = pltpu.get_barrier_semaphore()
    for device in partners:
        pl.semaphore_signal(barrier, inc=1, device_id=device, device_id_type=MESH)

    xt[...] = jnp.transpose(x_ref[...].astype(F32) * 2.0).astype(BF16)

    def largest(b, top):
        at_rows = pl.ds(pl.multiple_of(b * TILE, TILE), TILE)
        c = c_ref[at_rows, :]
        cf = c.astype(F32)
        norm = jnp.sum(cf * cf, axis=1, keepdims=True)
        cb[at_rows, :] = jnp.broadcast_to(norm, (TILE, 128))
        dots = jnp.dot(c, xt[...], preferred_element_type=F32)
        score = dots - norm
        return jnp.maximum(top, jnp.max(score.reshape(TILE // 8, 8, rows), axis=0))

    top8 = lax.fori_loop(0, cents // TILE, largest, jnp.full((8, rows), -jnp.inf, F32))
    top1 = jnp.max(top8, axis=0, keepdims=True)

    def weigh(b, total):
        at_rows = pl.ds(pl.multiple_of(b * TILE, TILE), TILE)
        dots = jnp.dot(c_ref[at_rows, :], xt[...], preferred_element_type=F32)
        norm = cb[at_rows, 0:1]
        e = jnp.exp((dots - norm) - top1)
        et[at_rows, :] = e.astype(BF16)
        return total + jnp.sum(e.reshape(TILE // 8, 8, rows), axis=0)

    total8 = lax.fori_loop(0, cents // TILE, weigh, jnp.zeros((8, rows), F32))
    total1 = jnp.sum(total8, axis=0, keepdims=True)

    lanes = rows // 8
    soft[cent, 0:8, :] = jnp.concatenate([top1[:, i * lanes:(i + 1) * lanes] for i in range(8)], axis=0)
    soft[cent, 8:16, :] = jnp.concatenate([total1[:, i * lanes:(i + 1) * lanes] for i in range(8)], axis=0)

    pl.semaphore_wait(barrier, len(partners))

    def soft_copy(slot, device):
        return pltpu.make_async_remote_copy(
            src_ref=soft.at[slot], dst_ref=soft.at[slot], send_sem=soft_send.at[slot], recv_sem=soft_recv.at[slot],
            device_id=device, device_id_type=MESH)

    soft_out = []
    for d in range(1, groups):
        peer = (cent + d) % groups
        copy = pltpu.make_async_remote_copy(
            src_ref=soft.at[cent], dst_ref=soft.at[cent], send_sem=soft_send.at[d], recv_sem=soft_recv.at[cent],
            device_id={"dp": dp, "cent": peer}, device_id_type=MESH)
        copy.start()
        soft_out.append(copy)
    for d in range(1, groups):
        peer = (cent + d) % groups
        soft_copy(peer, {"dp": dp, "cent": peer}).wait_recv()
    tops = [soft[g, 0:8, :] for g in range(groups)]
    top = functools.reduce(jnp.maximum, tops)
    total = jnp.zeros_like(top)
    for g in range(groups):
        total = total + soft[g, 8:16, :] * jnp.exp(tops[g] - top)
    log_ref[...] = top + jnp.log(total) - math.log(every_centroid)
    scale = jnp.exp(soft[cent, 0:8, :] - top) / total

    for i in range(8):
        column = jnp.transpose(jnp.broadcast_to(scale[i:i + 1, :], (lanes, lanes)))
        at_rows = slice(i * lanes, (i + 1) * lanes)
        x = x_ref[at_rows, :].astype(F32)
        xs[at_rows, 0:width] = jnp.concatenate(
            [(x[:, j:j + lanes] * column).astype(BF16) for j in range(0, width, lanes)], axis=1)
        high = column.astype(BF16)
        low = (column - high.astype(F32)).astype(BF16)
        lane = lax.broadcasted_iota(jnp.int32, (lanes, lanes), 1)
        xs[at_rows, width:width + lanes] = jnp.where(lane < lanes // 2, high.astype(F32), low.astype(F32)).astype(BF16)

    block_rows = cents // (2 * BLOCKS)
    urows, vrows = block_rows // 4, block_rows // 16
    zrows = vrows // 2

    eye = (lax.broadcasted_iota(jnp.int32, (128, 128), 0) == lax.broadcasted_iota(jnp.int32, (128, 128), 1))

    def sums(b, carry):
        start = pl.multiple_of(b * TILE, TILE)
        out = jnp.dot(et[pl.ds(start, TILE), :], xs[...], preferred_element_type=F32)
        part[pl.ds(start, TILE), :] = out[:, 0:width]
        c = out[:, width:width + 128]
        c = c + pltpu.roll(c, 64, 1)
        for i in range(TILE // 128):
            row = jnp.sum(jnp.where(eye, c[i * 128:(i + 1) * 128, :], 0.0), axis=0, keepdims=True)
            q[pl.ds(b * (TILE // 128) + i, 1), :] = row
        return carry

    started = []

    def remote(src, dst, k, device):
        return pltpu.make_async_remote_copy(
            src_ref=src, dst_ref=dst, send_sem=send.at[k], recv_sem=recv.at[k], device_id=device, device_id_type=MESH)

    def go(src, dst, k, device):
        copy = remote(src, dst, k, device)
        copy.start()
        started.append(copy)

    def arrived(dst, k):
        remote(dst, dst, k, at(z=1 - pz)).wait_recv()

    def rows_of(ref, start, size):
        return ref.at[pl.ds(pl.multiple_of(start, 8), size), :]

    def add(start, size, *others):
        here = pl.ds(pl.multiple_of(start, 8), size)
        value = part[here, :]
        for other in others:
            value = value + other[...]
        part[here, :] = value

    per = 22

    def ring_first(block, k, axis, position, base, size, rx):
        half = size // 2
        plus, minus = along(axis, 1), along(axis, 3)
        opposite, after, before = [base + ((position + d) % 4) * size for d in (2, 1, 3)]
        go(rows_of(part, opposite, half), rx.at[block, 0], k, plus)
        go(rows_of(part, opposite + half, half), rx.at[block, 1], k + 1, minus)
        go(rows_of(part, after + half, half), rx.at[block, 2], k + 2, plus)
        go(rows_of(part, before, half), rx.at[block, 3], k + 3, minus)

    def ring_second(block, k, axis, position, base, size, rx):
        half = size // 2
        plus, minus = along(axis, 1), along(axis, 3)
        after, before = [base + ((position + d) % 4) * size for d in (1, 3)]
        arrived(rx.at[block, 0], k)
        add(after, half, rx.at[block, 0])
        go(rows_of(part, after, half), rx.at[block, 4], k + 4, plus)
        arrived(rx.at[block, 1], k + 1)
        add(before + half, half, rx.at[block, 1])
        go(rows_of(part, before + half, half), rx.at[block, 5], k + 5, minus)

    def ring_third(block, k, position, base, size, rx):
        half = size // 2
        mine = base + position * size
        arrived(rx.at[block, 2], k + 2)
        arrived(rx.at[block, 3], k + 3)
        arrived(rx.at[block, 4], k + 4)
        add(mine, half, rx.at[block, 3], rx.at[block, 4])
        arrived(rx.at[block, 5], k + 5)
        add(mine + half, half, rx.at[block, 2], rx.at[block, 5])

    def spread_first(k, axis, position, base, size):
        mine = rows_of(sum_ref, base + position * size, size)
        go(mine, mine, k, along(axis, 1))
        go(mine, mine, k + 1, along(axis, 3))

    def spread_second(k, axis, position, base, size):
        half = size // 2
        before, after = [base + ((position + d) % 4) * size for d in (3, 1)]
        arrived(rows_of(sum_ref, before, size), k)
        there = rows_of(sum_ref, before, half)
        go(there, there, k + 2, along(axis, 1))
        arrived(rows_of(sum_ref, after, size), k + 1)
        there = rows_of(sum_ref, after + half, half)
        go(there, there, k + 3, along(axis, 3))

    def spread_third(k, position, base, size):
        half = size // 2
        opposite = base + ((position + 2) % 4) * size
        arrived(rows_of(sum_ref, opposite, half), k + 2)
        arrived(rows_of(sum_ref, opposite + half, half), k + 3)

    STAGES = 11

    def stage(h, s, number):
        block = h * BLOCKS + s
        base = block * block_rows
        k = block * per
        uaxis, vaxis = (0, 1) if h == 0 else (1, 0)
        u, v = (px, py) if h == 0 else (py, px)
        chunk = base + u * urows
        piece = chunk + v * vrows
        own, other = piece + pz * zrows, piece + (1 - pz) * zrows
        if number == 0:
            lax.fori_loop(base // TILE, (base + block_rows) // TILE, sums, 0)
            ring_first(block, k, uaxis, u, base, urows, rxu)
        elif number == 1:
            ring_second(block, k, uaxis, u, base, urows, rxu)
        elif number == 2:
            ring_third(block, k, u, base, urows, rxu)
            ring_first(block, k + 6, vaxis, v, chunk, vrows, rxv)
        elif number == 3:
            ring_second(block, k + 6, vaxis, v, chunk, vrows, rxv)
        elif number == 4:
            ring_third(block, k + 6, v, chunk, vrows, rxv)
            go(rows_of(part, other, zrows), rxz.at[block], k + 12, at(z=1 - pz))
        elif number == 5:
            arrived(rxz.at[block], k + 12)
            here = pl.ds(pl.multiple_of(own, 8), zrows)
            sum_ref[here, :] = part[here, :] + rxz[block]
            go(rows_of(sum_ref, own, zrows), rows_of(sum_ref, own, zrows), k + 13, at(z=1 - pz))
        elif number == 6:
            arrived(rows_of(sum_ref, other, zrows), k + 13)
            spread_first(k + 14, vaxis, v, chunk, vrows)
        elif number == 7:
            spread_second(k + 14, vaxis, v, chunk, vrows)
        elif number == 8:
            spread_third(k + 14, v, chunk, vrows)
            spread_first(k + 18, uaxis, u, base, urows)
        elif number == 9:
            spread_second(k + 18, uaxis, u, base, urows)
        elif number == 10:
            spread_third(k + 18, u, base, urows)

    def count_copy(level, source, k, device, slot):
        return pltpu.make_async_remote_copy(
            src_ref=source, dst_ref=qr.at[level, slot], send_sem=q_send.at[k], recv_sem=q_recv.at[level, slot],
            device_id=device, device_id_type=MESH)

    def counts_send(level):
        position = (px, py, pz)[level]
        qr[level, position] = q[...]
        for d in range(1, (NX, NY, NZ)[level]):
            device = along(level, d) if level < 2 else at(z=1 - pz)
            copy = count_copy(level, qr.at[level, position], level * 3 + d - 1, device, position)
            copy.start()
            started.append(copy)

    def counts_take(level):
        position, size = (px, py, pz)[level], (NX, NY, NZ)[level]
        for d in range(1, size):
            slot = (position + d) % size
            count_copy(level, qr.at[level, slot], level * 3, at(z=1 - pz), slot).wait_recv()
        value = qr[level, 0]
        for i in range(1, size):
            value = value + qr[level, i]
        if level < 2:
            q[...] = value
        else:
            count_ref[...] = value

    done = 0
    for s, number in stage_order(BLOCKS, STAGES):
        for h in (0, 1):
            stage(h, s, number)
        if number == 0:
            done += 1
            if done == BLOCKS:
                counts_send(0)
        if s == BLOCKS - 1 and number == 2:
            counts_take(0)
            counts_send(1)
        if s == BLOCKS - 1 and number == 4:
            counts_take(1)
            counts_send(2)
        if s == BLOCKS - 1 and number == 6:
            counts_take(2)
    for copy in soft_out + started:
        copy.wait_send()


def body(points, centroids):
    rows, width = points.shape
    cents = centroids.shape[0]
    groups = lax.axis_size("cent")
    block_rows = cents // (2 * BLOCKS)
    urows, vrows = block_rows // 4, block_rows // 16
    vmem = pl.BlockSpec(memory_space=pltpu.VMEM)
    messages = 2 * BLOCKS * 22
    sums, counts, log_evidence = pl.pallas_call(
        functools.partial(kernel, (rows, cents, width, groups)),
        out_shape=(
            jax.ShapeDtypeStruct((cents, width), F32),
            jax.ShapeDtypeStruct((cents // 128, 128), F32),
            jax.ShapeDtypeStruct((8, rows // 8), F32),
        ),
        in_specs=[vmem] * 2,
        out_specs=(vmem,) * 3,
        scratch_shapes=[
            pltpu.VMEM((width, rows), BF16),
            pltpu.VMEM((rows, width + 128), BF16),
            pltpu.VMEM((cents, rows), BF16),
            pltpu.VMEM((cents, 128), F32),
            pltpu.VMEM((cents, width), F32),
            pltpu.VMEM((2 * BLOCKS, 6, urows // 2, width), F32),
            pltpu.VMEM((2 * BLOCKS, 6, vrows // 2, width), F32),
            pltpu.VMEM((2 * BLOCKS, vrows // 2, width), F32),
            pltpu.VMEM((groups, 16, rows // 8), F32),
            pltpu.VMEM((cents // 128, 128), F32),
            pltpu.VMEM((3, 4, cents // 128, 128), F32),
            pltpu.SemaphoreType.DMA((groups,)),
            pltpu.SemaphoreType.DMA((groups,)),
            pltpu.SemaphoreType.DMA((9,)),
            pltpu.SemaphoreType.DMA((3, 4)),
            pltpu.SemaphoreType.DMA((messages,)),
            pltpu.SemaphoreType.DMA((messages,)),
        ],
        compiler_params=pltpu.CompilerParams(
            collective_id=0, has_side_effects=True, vmem_limit_bytes=58 * 1024 * 1024),
    )(points, centroids)
    counts = counts.reshape(cents)
    new_centroids = (sums + prior_mass * centroids.astype(F32)) / (counts + prior_mass)[:, None]
    return new_centroids, counts, log_evidence.reshape(rows)


def solution(mesh):
    return jax.shard_map(
        body,
        mesh=mesh,
        in_specs=(P("dp", None), P("cent", None)),
        out_specs=(P("cent", None), P("cent"), P("dp")),
        check_vma=False,
    )
```

time: 425 us -> 108 us (0.25)
  blocking collectives: 189 us -> 0 us
  waiting for transfers between devices: 182 us -> 0 us
  Pallas kernels: 0 us -> 101 us
  other arithmetic: 23.2 us -> 5.2 us
  between operations: 14.1 us -> 0.64 us
  matrix products: 12.6 us -> 0 us
    psum x1 -> x0, waiting for transfers between devices: 182 us -> none  [body(): all_sums, all_counts = lax.psum((sums, counts), 'dp')]
    psum x2 -> x0, blocking collectives: 169 us -> none  [the longest x1 155 us: body(): all_sums, all_counts = lax.psum((sums, counts), 'dp')]
    pallas_call x0 -> x1, Pallas kernels: none -> 101 us  [body(): pl.pallas_call(functools.partial(kernel, (rows, cents, width, groups)), o...]
    pmax x1 -> x0, blocking collectives: 19.9 us -> none  [body(): top = lax.pmax(jnp.max(score, axis=1), 'cent')]
    reduce_sum x2 -> x0, other arithmetic: 16.3 us -> none  [the longest x1 8.66 us: body(): counts = counts + jnp.sum(resp.astype(jnp.float32), axis=0)]
    dot_general x4 -> x0, matrix products: 12.6 us -> none  [the longest x2 7.92 us: body(): jnp.einsum('nd,kd->nk', piece, centroids, preferred_element_type=jnp.floa...]
  transfers between devices with their start and end apart: 1 -> 0, of which waited for: 1 -> 0; matrix products, arithmetic and copies ran while one was open for 0% -> 0% of each run, Pallas kernels for 0% -> 0%
where the time goes in v1:
time: 108 us
  Pallas kernels  101 us (94%)
  other arithmetic  5.2 us (5%)
  local copies, waits for them, and re-layouts  1.21 us (1%)
    pallas_call x1, Pallas kernels, body(): pl.pallas_call(functools.partial(kernel, (rows, cents, width, groups)), o...  101 us
    div x1, other arithmetic, body(): (sums + prior_mass * centroids.astype(F32)) / (counts + prior_mass)[:, None]  4.48 us

profile of v1, /device:TPU:8, one launch (start us, length us, event | category | flops | bytes accessed | tf_op | source)
XLA Modules:
  0.0 108.2 jit_solution(575207308981685545)
XLA Ops:
  0.6 101.2 %shard_map.49 = (f32[4096,256]{1,0:T(8,128)}, f32[32,128]{1,0:T(8,128)}, f32[8,128]{1,0:T(8,128)}) custom-call(bf16[1024,256]{1,0:T(8,128)(2,1)} %x_ref.1, bf16[4096,256]{1,0:T(8,128)(2,1)} %c_ref.1), custom_call_target="tpu_custom_call" | custom-call | tf_op jit(solution)/shard_map/pallas_call | solution.py:318
  101.8 0.7 broadcast_add_fusion
  102.5 0.0 copy-start
  102.5 0.0 copy-start.1
  102.5 4.5 %add_divide_fusion = f32[4096,256]{1,0:T(8,128)} fusion(f32[4096,256]{1,0:T(8,128)} %get-tuple-element.6, bf16[4096,256]{1,0:T(8,128)(2,1)} %c_ref.1, f32[4096]{0:T(1024)S(1)} %broadcast_add_fusion), kind=kLoop, calls=%fused_computation | loop fusion | flops 4194304 | bytes 10502144 | tf_op jit(solution)/shard_map/div | solution.py:350
  107.0 0.0 copy-done
  107.0 0.6 copy.7
  107.6 0.0 copy-done.1
  107.6 0.6 copy.8
Async XLA Ops:
  102.5 4.5 %copy-start = (f32[32,128]{1,0:T(8,128)S(1)}, f32[32,128]{1,0:T(8,128)}, u32[]{:S(2)}) copy-start(f32[32,128]{1,0:T(8,128)} %get-tuple-element.7) | copy-start | bytes 49156
  102.5 5.1 %copy-start.1 = (f32[8,128]{1,0:T(8,128)S(1)}, f32[8,128]{1,0:T(8,128)}, u32[]{:S(2)}) copy-start(f32[8,128]{1,0:T(8,128)} %get-tuple-element.8) | copy-start | bytes 12292

commit v2 on v0

v2 whole, which is shorter than its diff:
```python
import functools
import math

import jax
import jax.numpy as jnp
from jax import lax
from jax.experimental import pallas as pl
from jax.experimental.pallas import tpu as pltpu
from jax.sharding import PartitionSpec as P

MESH = pl.DeviceIdType.MESH
prior_mass = 0.5

NX, NY, NZ = 4, 4, 2
TILE = 512
F32, BF16 = jnp.float32, jnp.bfloat16

BLOCKS = (
    (512, 0, True),
    (512, 1, True),
    (512, 0, False),
    (512, 1, False),
    (1024, 0, False),
    (1024, 1, False),
)
ORDER = (
    2, 1, 5, 0, 4, 3, 6, 2, 5, 4, 1, 3, 6, 2, 0, 5, 1, 4, 3, 0, 6, 2, 5, 1, 4, 3, 0, 6, 2, 5, 1, 4, 3, 0, 2, 1, 5, 4,
    3, 0, 2, 1, 5, 4, 0, 3, 2, 1, 5, 3, 4, 0, 2, 1, 5, 3, 4, 0, 1, 2, 5, 1, 4, 0, 3, 2, 5, 0, 3, 4,
)


def programs(o, px, py, pz):
    result = []
    base = 0
    for index, (rows, h, zfirst) in enumerate(BLOCKS):
        result.append(block_program(o, index, base, rows, h, zfirst, px, py, pz))
        base += rows
    result.append(count_program(o))
    return result


def block_program(o, index, base, rows, h, zfirst, px, py, pz):
    names = (("x+", "x-"), ("y+", "y-"))
    udir, vdir = names[h], names[1 - h]
    u, v = ((px, py), (py, px))[h]
    ubase = base + pz * (rows // 2) if zfirst else base
    span = rows // 2 if zfirst else rows
    urows, vrows = span // 4, span // 16
    zrows = vrows // 2
    chunk = ubase + u * urows
    piece = chunk + v * vrows
    own, other = piece + pz * zrows, piece + (1 - pz) * zrows

    def key(tag, level):
        return (index, tag, level)

    def first(level, d, p, start, size):
        half = size // 2
        opposite, after, before = [start + ((p + i) % 4) * size for i in (2, 1, 3)]
        o.send_part(d[0], opposite, half, key("o+", level))
        o.send_part(d[1], opposite + half, half, key("o-", level))
        o.send_part(d[0], after + half, half, key("d+", level))
        o.send_part(d[1], before, half, key("d-", level))

    def second(level, d, p, start, size):
        half = size // 2
        after, before = [start + ((p + i) % 4) * size for i in (1, 3)]
        o.wait(key("o+", level), half)
        o.add(after, half, [key("o+", level)])
        o.send_part(d[0], after, half, key("c+", level))
        o.wait(key("o-", level), half)
        o.add(before + half, half, [key("o-", level)])
        o.send_part(d[1], before + half, half, key("c-", level))

    def third(level, p, start, size, final=False):
        half = size // 2
        mine = start + p * size
        for tag in ("d+", "d-", "c+", "c-"):
            o.wait(key(tag, level), half)
        o.add(mine, half, [key("d-", level), key("c+", level)], final)
        o.add(mine + half, half, [key("d+", level), key("c-", level)], final)

    def spread_first(level, d, p, start, size):
        o.send_sum(d[0], start + p * size, size, key("f+", level))
        o.send_sum(d[1], start + p * size, size, key("f-", level))

    def spread_second(level, d, p, start, size):
        half = size // 2
        before, after = [start + ((p + i) % 4) * size for i in (3, 1)]
        o.wait_sum(key("f+", level), before, size)
        o.send_sum(d[0], before, half, key("g+", level))
        o.wait_sum(key("f-", level), after, size)
        o.send_sum(d[1], after + half, half, key("g-", level))

    def spread_third(level, p, start, size):
        half = size // 2
        opposite = start + ((p + 2) % 4) * size
        o.wait_sum(key("g+", level), opposite, half)
        o.wait_sum(key("g-", level), opposite + half, half)

    def zsend(n):
        place = ubase + ((u + n) % 4) * urows
        o.send_sum("z", place, urows, key("h", n))

    def zwait(n):
        place = base + (1 - pz) * (rows // 2) + ((u + n) % 4) * urows
        o.wait_sum(key("h", n), place, urows)

    if zfirst:
        def s0():
            o.sums(base, rows)
            o.send_part("z", base + (1 - pz) * span, span, key("z", 0))

        def s1():
            o.wait(key("z", 0), span)
            o.add(ubase, span, [key("z", 0)])
            first(0, udir, u, ubase, urows)

        def s5():
            third(1, v, chunk, vrows, True)
            spread_first(1, vdir, v, chunk, vrows)

        def s7():
            spread_third(1, v, chunk, vrows)
            spread_first(0, udir, u, ubase, urows)
            zsend(0)

        def s8():
            spread_second(0, udir, u, ubase, urows)
            zsend(1)
            zsend(3)

        def s9():
            spread_third(0, u, ubase, urows)
            zsend(2)

        return [
            s0, s1,
            lambda: second(0, udir, u, ubase, urows),
            lambda: (third(0, u, ubase, urows), first(1, vdir, v, chunk, vrows)),
            lambda: second(1, vdir, v, chunk, vrows),
            s5,
            lambda: spread_second(1, vdir, v, chunk, vrows),
            s7, s8, s9,
            lambda: [zwait(n) for n in range(4)],
        ]

    def t4():
        third(1, v, chunk, vrows)
        o.send_part("z", other, zrows, key("z", 0))

    def t5():
        o.wait(key("z", 0), zrows)
        o.add(own, zrows, [key("z", 0)], True)
        o.send_sum("z", own, zrows, key("h", 0))

    def t6():
        o.wait_sum(key("h", 0), other, zrows)
        spread_first(1, vdir, v, chunk, vrows)

    return [
        lambda: (o.sums(base, rows), first(0, udir, u, base, urows)),
        lambda: second(0, udir, u, base, urows),
        lambda: (third(0, u, base, urows), first(1, vdir, v, chunk, vrows)),
        lambda: second(1, vdir, v, chunk, vrows),
        t4, t5, t6,
        lambda: spread_second(1, vdir, v, chunk, vrows),
        lambda: (spread_third(1, v, chunk, vrows), spread_first(0, udir, u, base, urows)),
        lambda: spread_second(0, udir, u, base, urows),
        lambda: spread_third(0, u, base, urows),
    ]


def count_program(o):
    return [
        lambda: (o.counts(), o.count_send(0)),
        lambda: (o.count_take(0), o.count_send(1)),
        lambda: (o.count_take(1), o.count_send(2)),
        lambda: o.count_take(2),
    ]


class Messages:
    def __init__(self):
        self.ids, self.places, self.rows = {}, {}, 0

    def number(self, key):
        return self.ids.setdefault(key, len(self.ids))

    def send_part(self, direction, start, size, key):
        self.number(key)
        self.places[key] = (self.rows, size)
        self.rows += size

    def send_sum(self, direction, start, size, key):
        self.number(key)

    def wait(self, *_):
        pass

    wait_sum = add = sums = counts = count_send = count_take = wait


def messages():
    found = Messages()
    for stages in programs(found, 0, 0, 0):
        for run in stages:
            run()
    return found


def kernel(sizes, x_ref, c_ref, sum_ref, count_ref, log_ref,
           xt, xs, et, cb, part, rx, scales, soft, q, qr,
           soft_send, soft_recv, q_send, q_recv, send, recv):
    rows, cents, width, groups = sizes
    every_centroid = cents * groups
    dp, cent = lax.axis_index("dp"), lax.axis_index("cent")
    px, py, pz = dp // (NY * NZ), (dp // NZ) % NY, dp % NZ

    def at(x=None, y=None, z=None):
        x = px if x is None else x
        y = py if y is None else y
        z = pz if z is None else z
        return {"dp": (x * NY + y) * NZ + z, "cent": cent}

    def along(axis, offset):
        if axis == 0:
            return at(x=(px + offset) % NX)
        return at(y=(py + offset) % NY)

    partners = [along(a, d) for a in (0, 1) for d in (1, 2, 3)] + [at(z=1 - pz)]
    partners += [{"dp": dp, "cent": (cent + d) % groups} for d in range(1, groups)]
    barrier = pltpu.get_barrier_semaphore()
    for device in partners:
        pl.semaphore_signal(barrier, inc=1, device_id=device, device_id_type=MESH)

    xt[...] = jnp.transpose(x_ref[...].astype(F32) * 2.0).astype(BF16)

    def largest(b, top):
        at_rows = pl.ds(pl.multiple_of(b * TILE, TILE), TILE)
        c = c_ref[at_rows, :]
        cf = c.astype(F32)
        norm = jnp.sum(cf * cf, axis=1, keepdims=True)
        cb[at_rows, :] = jnp.broadcast_to(norm, (TILE, 128))
        dots = jnp.dot(c, xt[...], preferred_element_type=F32)
        score = dots - norm
        return jnp.maximum(top, jnp.max(score.reshape(TILE // 8, 8, rows), axis=0))

    top8 = lax.fori_loop(0, cents // TILE, largest, jnp.full((8, rows), -jnp.inf, F32))
    top1 = jnp.max(top8, axis=0, keepdims=True)

    def weigh(b, total):
        at_rows = pl.ds(pl.multiple_of(b * TILE, TILE), TILE)
        dots = jnp.dot(c_ref[at_rows, :], xt[...], preferred_element_type=F32)
        norm = cb[at_rows, 0:1]
        e = jnp.exp((dots - norm) - top1)
        et[at_rows, :] = e.astype(BF16)
        return total + jnp.sum(e.reshape(TILE // 8, 8, rows), axis=0)

    total8 = lax.fori_loop(0, cents // TILE, weigh, jnp.zeros((8, rows), F32))
    total1 = jnp.sum(total8, axis=0, keepdims=True)

    lanes = rows // 8
    soft[cent, 0:8, :] = jnp.concatenate([top1[:, i * lanes:(i + 1) * lanes] for i in range(8)], axis=0)
    soft[cent, 8:16, :] = jnp.concatenate([total1[:, i * lanes:(i + 1) * lanes] for i in range(8)], axis=0)

    pl.semaphore_wait(barrier, len(partners))

    def soft_copy(slot, device):
        return pltpu.make_async_remote_copy(
            src_ref=soft.at[slot], dst_ref=soft.at[slot], send_sem=soft_send.at[slot], recv_sem=soft_recv.at[slot],
            device_id=device, device_id_type=MESH)

    soft_out = []
    for d in range(1, groups):
        peer = (cent + d) % groups
        copy = pltpu.make_async_remote_copy(
            src_ref=soft.at[cent], dst_ref=soft.at[cent], send_sem=soft_send.at[d], recv_sem=soft_recv.at[cent],
            device_id={"dp": dp, "cent": peer}, device_id_type=MESH)
        copy.start()
        soft_out.append(copy)
    for d in range(1, groups):
        peer = (cent + d) % groups
        soft_copy(peer, {"dp": dp, "cent": peer}).wait_recv()
    tops = [soft[g, 0:8, :] for g in range(groups)]
    top = functools.reduce(jnp.maximum, tops)
    total = jnp.zeros_like(top)
    for g in range(groups):
        total = total + soft[g, 8:16, :] * jnp.exp(tops[g] - top)
    log_ref[...] = top + jnp.log(total) - math.log(every_centroid)
    scale = jnp.exp(soft[cent, 0:8, :] - top) / total

    for i in range(8):
        column = jnp.transpose(jnp.broadcast_to(scale[i:i + 1, :], (lanes, lanes)))
        at_rows = slice(i * lanes, (i + 1) * lanes)
        x = x_ref[at_rows, :].astype(F32)
        xs[at_rows, :] = jnp.concatenate(
            [(x[:, j:j + lanes] * column).astype(BF16) for j in range(0, width, lanes)], axis=1)
    high = scale.astype(BF16).astype(F32)
    low = scale - high
    filler = jnp.zeros((14, lanes), F32)
    for i in range(8):
        both = jnp.concatenate([high[i:i + 1, :], low[i:i + 1, :], filler], axis=0)
        scales[:, i * lanes:(i + 1) * lanes] = both.astype(BF16)

    started = []

    found = messages()

    def remote(src, dst, k, device):
        return pltpu.make_async_remote_copy(
            src_ref=src, dst_ref=dst, send_sem=send.at[k], recv_sem=recv.at[k], device_id=device, device_id_type=MESH)

    devices = {"x+": along(0, 1), "x-": along(0, 3), "y+": along(1, 1), "y-": along(1, 3), "z": at(z=1 - pz)}

    def rows_of(ref, start, size):
        return ref.at[pl.ds(start if isinstance(start, int) else pl.multiple_of(start, 8), size), :]

    class Issue:
        def sums(self, start, size):
            tile = min(size, TILE)
            for i in range(start, start + size, tile):
                part[i:i + tile, :] = jnp.dot(et[i:i + tile, :], xs[...], preferred_element_type=F32)

        def send_part(self, direction, start, size, key):
            copy = remote(rows_of(part, start, size), rows_of(rx, found.places[key][0], size), found.number(key), devices[direction])
            copy.start()
            started.append(copy)

        def send_sum(self, direction, start, size, key):
            here = rows_of(sum_ref, start, size)
            copy = remote(here, here, found.number(key), devices[direction])
            copy.start()
            started.append(copy)

        def wait(self, key, size):
            here = rows_of(rx, found.places[key][0], size)
            remote(here, here, found.number(key), devices["z"]).wait_recv()

        def wait_sum(self, key, start, size):
            here = rows_of(sum_ref, start, size)
            remote(here, here, found.number(key), devices["z"]).wait_recv()

        def add(self, start, size, keys, final=False):
            here = pl.ds(pl.multiple_of(start, 8), size)
            value = part[here, :]
            for key in keys:
                place = found.places[key][0]
                value = value + rx[place:place + size, :]
            if final:
                sum_ref[here, :] = value
            else:
                part[here, :] = value

        def counts(self):
            def one(b, carry):
                start = pl.multiple_of(b * TILE, TILE)
                out = lax.dot_general(scales[...], et[pl.ds(start, TILE), :], (((1,), (1,)), ((), ())),
                                      preferred_element_type=F32)
                row = out[0:1, :] + out[1:2, :]
                for i in range(TILE // 128):
                    q[pl.ds(b * (TILE // 128) + i, 1), :] = row[:, i * 128:(i + 1) * 128]
                return carry

            lax.fori_loop(0, cents // TILE, one, 0)

        def copy(self, level, source, k, device, slot):
            return pltpu.make_async_remote_copy(
                src_ref=source, dst_ref=qr.at[level, slot], send_sem=q_send.at[k], recv_sem=q_recv.at[level, slot],
                device_id=device, device_id_type=MESH)

        def count_send(self, level):
            position = (px, py, pz)[level]
            qr[level, position] = q[...]
            for d in range(1, (NX, NY, NZ)[level]):
                device = along(level, d) if level < 2 else at(z=1 - pz)
                copy = self.copy(level, qr.at[level, position], level * 3 + d - 1, device, position)
                copy.start()
                started.append(copy)

        def count_take(self, level):
            position, size = (px, py, pz)[level], (NX, NY, NZ)[level]
            for d in range(1, size):
                slot = (position + d) % size
                self.copy(level, qr.at[level, slot], level * 3, at(z=1 - pz), slot).wait_recv()
            value = qr[level, 0]
            for i in range(1, size):
                value = value + qr[level, i]
            if level < 2:
                q[...] = value
            else:
                count_ref[...] = value

    stages = [iter(p) for p in programs(Issue(), px, py, pz)]
    for block in ORDER:
        next(stages[block])()
    for copy in soft_out + started:
        copy.wait_send()


def body(points, centroids):
    rows, width = points.shape
    cents = centroids.shape[0]
    groups = lax.axis_size("cent")
    found = messages()
    vmem = pl.BlockSpec(memory_space=pltpu.VMEM)
    sums, counts, log_evidence = pl.pallas_call(
        functools.partial(kernel, (rows, cents, width, groups)),
        out_shape=(
            pltpu.VMEM((cents, width), F32),
            pltpu.VMEM((cents // 128, 128), F32),
            pltpu.VMEM((8, rows // 8), F32),
        ),
        in_specs=[vmem] * 2,
        out_specs=(vmem,) * 3,
        scratch_shapes=[
            pltpu.VMEM((width, rows), BF16),
            pltpu.VMEM((rows, width), BF16),
            pltpu.VMEM((cents, rows), BF16),
            pltpu.VMEM((cents, 128), F32),
            pltpu.VMEM((cents, width), F32),
            pltpu.VMEM((found.rows, width), F32),
            pltpu.VMEM((16, rows), BF16),
            pltpu.VMEM((groups, 16, rows // 8), F32),
            pltpu.VMEM((cents // 128, 128), F32),
            pltpu.VMEM((3, 4, cents // 128, 128), F32),
            pltpu.SemaphoreType.DMA((groups,)),
            pltpu.SemaphoreType.DMA((groups,)),
            pltpu.SemaphoreType.DMA((9,)),
            pltpu.SemaphoreType.DMA((3, 4)),
            pltpu.SemaphoreType.DMA((len(found.ids),)),
            pltpu.SemaphoreType.DMA((len(found.ids),)),
        ],
        compiler_params=pltpu.CompilerParams(
            collective_id=0, has_side_effects=True, vmem_limit_bytes=58 * 1024 * 1024),
    )(points, centroids)
    counts = counts.reshape(cents)
    new_centroids = (sums + prior_mass * centroids.astype(F32)) / (counts + prior_mass)[:, None]
    return new_centroids, counts, log_evidence.reshape(rows)


def solution(mesh):
    return jax.shard_map(
        body,
        mesh=mesh,
        in_specs=(P("dp", None), P("cent", None)),
        out_specs=(P("cent", None), P("cent"), P("dp")),
        check_vma=False,
    )
```

time: 425 us -> 81.7 us (0.19)
  blocking collectives: 189 us -> 0 us
  waiting for transfers between devices: 182 us -> 0 us
  Pallas kernels: 0 us -> 75.7 us
  other arithmetic: 23.2 us -> 3.59 us
  between operations: 14.1 us -> 0.64 us
  matrix products: 12.6 us -> 0 us
    psum x1 -> x0, waiting for transfers between devices: 182 us -> none  [body(): all_sums, all_counts = lax.psum((sums, counts), 'dp')]
    psum x2 -> x0, blocking collectives: 169 us -> none  [the longest x1 155 us: body(): all_sums, all_counts = lax.psum((sums, counts), 'dp')]
    pallas_call x0 -> x1, Pallas kernels: none -> 75.7 us  [body(): pl.pallas_call(functools.partial(kernel, (rows, cents, width, groups)), o...]
    pmax x1 -> x0, blocking collectives: 19.9 us -> none  [body(): top = lax.pmax(jnp.max(score, axis=1), 'cent')]
    reduce_sum x2 -> x0, other arithmetic: 16.3 us -> none  [the longest x1 8.66 us: body(): counts = counts + jnp.sum(resp.astype(jnp.float32), axis=0)]
    dot_general x4 -> x0, matrix products: 12.6 us -> none  [the longest x2 7.92 us: body(): jnp.einsum('nd,kd->nk', piece, centroids, preferred_element_type=jnp.floa...]
  transfers between devices with their start and end apart: 1 -> 0, of which waited for: 1 -> 0; matrix products, arithmetic and copies ran while one was open for 0% -> 0% of each run, Pallas kernels for 0% -> 0%
where the time goes in v2:
time: 81.7 us; the launch traced here: 81.2 us
  Pallas kernels  75.7 us (93%)
  other arithmetic  3.59 us (4%)
  local copies, waits for them, and re-layouts  1.2 us (1%)
    pallas_call x1, Pallas kernels, body(): pl.pallas_call(functools.partial(kernel, (rows, cents, width, groups)), o...  75.7 us
    div x1, other arithmetic, body(): (sums + prior_mass * centroids.astype(F32)) / (counts + prior_mass)[:, None]  3.58 us

profile of v2, /device:TPU:8, one launch (start us, length us, event | category | flops | bytes accessed | tf_op | source)
XLA Modules:
  0.0 81.2 jit_solution(17759311220152095814)
XLA Ops:
  0.6 75.7 %shard_map.49 = (f32[4096,256]{1,0:T(8,128)S(1)}, f32[32,128]{1,0:T(8,128)S(1)}, f32[8,128]{1,0:T(8,128)S(1)}) custom-call(bf16[1024,256]{1,0:T(8,128)(2,1)} %x_ref.1, bf16[4096,256]{1,0:T(8,128)(2,1)} %c_ref.1), custom_call_target="tpu_custom_call" | custom-call | tf_op jit(solution)/shard_map/pallas_call | solution.py:407
  76.4 0.6 copy.8
  77.0 0.6 copy.7
  77.6 3.6 %add_divide_fusion = f32[4096,256]{1,0:T(8,128)} fusion(f32[4096,256]{1,0:T(8,128)S(1)} %get-tuple-element.6, bf16[4096,256]{1,0:T(8,128)(2,1)} %c_ref.1, f32[4096]{0:T(1024)S(1)} %broadcast_add_fusion), kind=kLoop, calls=%fused_computation | loop fusion | flops 4194304 | bytes 10502144 | tf_op jit(solution)/shard_map/div | solution.py:438
  (1 shorter events, 0.0 us)

commit v3 on v2

--- a/solution.py
+++ b/solution.py
@@ -13,6 +13,8 @@
 
 NX, NY, NZ = 4, 4, 2
 TILE = 512
+LOAD = 1024
+GROUP = 512
 F32, BF16 = jnp.float32, jnp.bfloat16
 
 BLOCKS = (
@@ -24,9 +26,14 @@
     (1024, 1, False),
 )
 ORDER = (
-    2, 1, 5, 0, 4, 3, 6, 2, 5, 4, 1, 3, 6, 2, 0, 5, 1, 4, 3, 0, 6, 2, 5, 1, 4, 3, 0, 6, 2, 5, 1, 4, 3, 0, 2, 1, 5, 4,
-    3, 0, 2, 1, 5, 4, 0, 3, 2, 1, 5, 3, 4, 0, 2, 1, 5, 3, 4, 0, 1, 2, 5, 1, 4, 0, 3, 2, 5, 0, 3, 4,
+    2, 3, 0, 4, 5, 3, 1, 4, 5, 2, 6, 0, 3, 4, 1, 5, 2, 0, 4, 1, 3, 5, 2, 4, 0, 3, 1, 6, 5, 2, 0, 4, 1, 3, 2, 5, 0, 1,
+    4, 3, 0, 1, 5, 2, 3, 4, 0, 1, 2, 5, 3, 4, 6, 0, 2, 5, 6, 1, 4, 3, 0, 5, 1, 2, 0, 3, 4, 1, 5, 2,
 )
+
+
+def split(size):
+    half = size // 16 * 8
+    return half, size - half
 
 
 def programs(o, px, py, pz):
@@ -55,48 +62,48 @@
         return (index, tag, level)
 
     def first(level, d, p, start, size):
-        half = size // 2
+        half, rest = split(size)
         opposite, after, before = [start + ((p + i) % 4) * size for i in (2, 1, 3)]
         o.send_part(d[0], opposite, half, key("o+", level))
-        o.send_part(d[1], opposite + half, half, key("o-", level))
-        o.send_part(d[0], after + half, half, key("d+", level))
+        o.send_part(d[1], opposite + half, rest, key("o-", level))
+        o.send_part(d[0], after + half, rest, key("d+", level))
         o.send_part(d[1], before, half, key("d-", level))
 
     def second(level, d, p, start, size):
-        half = size // 2
+        half, rest = split(size)
         after, before = [start + ((p + i) % 4) * size for i in (1, 3)]
         o.wait(key("o+", level), half)
         o.add(after, half, [key("o+", level)])
         o.send_part(d[0], after, half, key("c+", level))
-        o.wait(key("o-", level), half)
-        o.add(before + half, half, [key("o-", level)])
-        o.send_part(d[1], before + half, half, key("c-", level))
+        o.wait(key("o-", level), rest)
+        o.add(before + half, rest, [key("o-", level)])
+        o.send_part(d[1], before + half, rest, key("c-", level))
 
     def third(level, p, start, size, final=False):
-        half = size // 2
+        half, rest = split(size)
         mine = start + p * size
-        for tag in ("d+", "d-", "c+", "c-"):
-            o.wait(key(tag, level), half)
+        for tag, part in (("d+", rest), ("d-", half), ("c+", half), ("c-", rest)):
+            o.wait(key(tag, level), part)
         o.add(mine, half, [key("d-", level), key("c+", level)], final)
-        o.add(mine + half, half, [key("d+", level), key("c-", level)], final)
+        o.add(mine + half, rest, [key("d+", level), key("c-", level)], final)
 
     def spread_first(level, d, p, start, size):
         o.send_sum(d[0], start + p * size, size, key("f+", level))
         o.send_sum(d[1], start + p * size, size, key("f-", level))
 
     def spread_second(level, d, p, start, size):
-        half = size // 2
+        half, rest = split(size)
         before, after = [start + ((p + i) % 4) * size for i in (3, 1)]
         o.wait_sum(key("f+", level), before, size)
         o.send_sum(d[0], before, half, key("g+", level))
         o.wait_sum(key("f-", level), after, size)
-        o.send_sum(d[1], after + half, half, key("g-", level))
+        o.send_sum(d[1], after + half, rest, key("g-", level))
 
     def spread_third(level, p, start, size):
-        half = size // 2
+        half, rest = split(size)
         opposite = start + ((p + 2) % 4) * size
         o.wait_sum(key("g+", level), opposite, half)
-        o.wait_sum(key("g-", level), opposite + half, half)
+        o.wait_sum(key("g-", level), opposite + half, rest)
 
     def zsend(n):
         place = ubase + ((u + n) % 4) * urows
@@ -142,7 +149,7 @@
             s5,
             lambda: spread_second(1, vdir, v, chunk, vrows),
             s7, s8, s9,
-            lambda: [zwait(n) for n in range(4)],
+            lambda: ([zwait(n) for n in range(4)], o.norm(base, rows)),
         ]
 
     def t4():
@@ -167,7 +174,7 @@
         lambda: spread_second(1, vdir, v, chunk, vrows),
         lambda: (spread_third(1, v, chunk, vrows), spread_first(0, udir, u, base, urows)),
         lambda: spread_second(0, udir, u, base, urows),
-        lambda: spread_third(0, u, base, urows),
+        lambda: (spread_third(0, u, base, urows), o.norm(base, rows)),
     ]
 
 
@@ -198,7 +205,7 @@
     def wait(self, *_):
         pass
 
-    wait_sum = add = sums = counts = count_send = count_take = wait
+    wait_sum = add = norm = sums = counts = count_send = count_take = wait
 
 
 def messages():
@@ -209,9 +216,9 @@
     return found
 
 
-def kernel(sizes, x_ref, c_ref, sum_ref, count_ref, log_ref,
-           xt, xs, et, cb, part, rx, scales, soft, q, qr,
-           soft_send, soft_recv, q_send, q_recv, send, recv):
+def kernel(sizes, x_ref, c_hbm, out_ref, count_ref, log_ref,
+           c_ref, sum_ref, score, xt, xs, et, cb, part, rx, scales, soft, q, qr,
+           c_sem, soft_send, soft_recv, q_send, q_recv, send, recv):
     rows, cents, width, groups = sizes
     every_centroid = cents * groups
     dp, cent = lax.axis_index("dp"), lax.axis_index("cent")
@@ -234,31 +241,48 @@
     for device in partners:
         pl.semaphore_signal(barrier, inc=1, device_id=device, device_id_type=MESH)
 
+    loads = []
+    for i in range(cents // LOAD):
+        here = slice(i * LOAD, (i + 1) * LOAD)
+        loads.append(pltpu.make_async_copy(c_hbm.at[here, :], c_ref.at[here, :], c_sem.at[i]))
+        loads[-1].start()
+
     xt[...] = jnp.transpose(x_ref[...].astype(F32) * 2.0).astype(BF16)
 
-    def largest(b, top):
-        at_rows = pl.ds(pl.multiple_of(b * TILE, TILE), TILE)
-        c = c_ref[at_rows, :]
-        cf = c.astype(F32)
-        norm = jnp.sum(cf * cf, axis=1, keepdims=True)
-        cb[at_rows, :] = jnp.broadcast_to(norm, (TILE, 128))
-        dots = jnp.dot(c, xt[...], preferred_element_type=F32)
-        score = dots - norm
-        return jnp.maximum(top, jnp.max(score.reshape(TILE // 8, 8, rows), axis=0))
-
-    top8 = lax.fori_loop(0, cents // TILE, largest, jnp.full((8, rows), -jnp.inf, F32))
-    top1 = jnp.max(top8, axis=0, keepdims=True)
-
-    def weigh(b, total):
-        at_rows = pl.ds(pl.multiple_of(b * TILE, TILE), TILE)
-        dots = jnp.dot(c_ref[at_rows, :], xt[...], preferred_element_type=F32)
-        norm = cb[at_rows, 0:1]
-        e = jnp.exp((dots - norm) - top1)
-        et[at_rows, :] = e.astype(BF16)
-        return total + jnp.sum(e.reshape(TILE // 8, 8, rows), axis=0)
-
-    total8 = lax.fori_loop(0, cents // TILE, weigh, jnp.zeros((8, rows), F32))
-    total1 = jnp.sum(total8, axis=0, keepdims=True)
+    tops, totals = [], []
+    for g in range(rows // GROUP + 1):
+        def visit(b, carry, g=g):
+            top, total = carry
+            here = pl.ds(pl.multiple_of(b * LOAD, LOAD), LOAD)
+            if g < rows // GROUP:
+                c = c_ref[here, :]
+                if g == 0:
+                    cf = c.astype(F32)
+                    norm = jnp.sum(cf * cf, axis=1, keepdims=True)
+                    cb[here, :] = jnp.broadcast_to(norm, (LOAD, 128))
+                else:
+                    norm = cb[here, 0:1]
+                value = jnp.dot(c, xt[:, g * GROUP:(g + 1) * GROUP], preferred_element_type=F32) - norm
+                score[g % 2, here, :] = value
+                top = jnp.maximum(top, jnp.max(value.reshape(LOAD // 8, 8, GROUP), axis=0))
+            if g > 0:
+                e = jnp.exp(score[(g - 1) % 2, here, :] - tops[g - 1])
+                et[here, (g - 1) * GROUP:g * GROUP] = e.astype(BF16)
+                total = total + jnp.sum(e.reshape(LOAD // 8, 8, GROUP), axis=0)
+            return top, total
+
+        carry = (jnp.full((8, GROUP), -jnp.inf, F32), jnp.zeros((8, GROUP), F32))
+        if g == 0:
+            for b in range(cents // LOAD):
+                loads[b].wait()
+                carry = visit(b, carry)
+        else:
+            carry = lax.fori_loop(0, cents // LOAD, visit, carry)
+        if g < rows // GROUP:
+            tops.append(jnp.max(carry[0], axis=0, keepdims=True))
+        if g > 0:
+            totals.append(jnp.sum(carry[1], axis=0, keepdims=True))
+    top1, total1 = jnp.concatenate(tops, axis=1), jnp.concatenate(totals, axis=1)
 
     lanes = rows // 8
     soft[cent, 0:8, :] = jnp.concatenate([top1[:, i * lanes:(i + 1) * lanes] for i in range(8)], axis=0)
@@ -390,12 +414,39 @@
                 q[...] = value
             else:
                 count_ref[...] = value
+                inverse = 1.0 / (value + prior_mass)
+                for i in range(cents // 128):
+                    cb[i * 128:(i + 1) * 128, :] = jnp.transpose(jnp.broadcast_to(inverse[i:i + 1, :], (128, 128)))
+
+        def norm(self, start, size):
+            def one(b, carry):
+                here = pl.ds(pl.multiple_of(start + b * 128, 128), 128)
+                inverse = cb[here, :]
+                for j in range(0, width, 128):
+                    value = sum_ref[here, j:j + 128] + prior_mass * c_ref[here, j:j + 128].astype(F32)
+                    out_ref[here, j:j + 128] = value * inverse
+                return carry
+
+            lax.fori_loop(0, size // 128, one, 0)
 
     stages = [iter(p) for p in programs(Issue(), px, py, pz)]
     for block in ORDER:
         next(stages[block])()
     for copy in soft_out + started:
         copy.wait_send()
+
+
+def put_out(centroids, counts, log, centroids_out, counts_out, log_out, sem):
+    pairs = [(counts, counts_out), (log, log_out)]
+    quarter = centroids.shape[0] // 4
+    for i in range(4):
+        here = slice(i * quarter, (i + 1) * quarter)
+        pairs.append((centroids.at[here, :], centroids_out.at[here, :]))
+    copies = [pltpu.make_async_copy(a, b, sem.at[i]) for i, (a, b) in enumerate(pairs)]
+    for copy in copies:
+        copy.start()
+    for copy in copies:
+        copy.wait()
 
 
 def body(points, centroids):
@@ -404,16 +455,19 @@
     groups = lax.axis_size("cent")
     found = messages()
     vmem = pl.BlockSpec(memory_space=pltpu.VMEM)
-    sums, counts, log_evidence = pl.pallas_call(
+    results = pl.pallas_call(
         functools.partial(kernel, (rows, cents, width, groups)),
         out_shape=(
             pltpu.VMEM((cents, width), F32),
             pltpu.VMEM((cents // 128, 128), F32),
             pltpu.VMEM((8, rows // 8), F32),
         ),
-        in_specs=[vmem] * 2,
+        in_specs=[vmem, pl.BlockSpec(memory_space=pl.ANY)],
         out_specs=(vmem,) * 3,
         scratch_shapes=[
+            pltpu.VMEM((cents, width), BF16),
+            pltpu.VMEM((cents, width), F32),
+            pltpu.VMEM((2, cents, GROUP), F32),
             pltpu.VMEM((width, rows), BF16),
             pltpu.VMEM((rows, width), BF16),
             pltpu.VMEM((cents, rows), BF16),
@@ -424,6 +478,7 @@
             pltpu.VMEM((groups, 16, rows // 8), F32),
             pltpu.VMEM((cents // 128, 128), F32),
             pltpu.VMEM((3, 4, cents // 128, 128), F32),
+            pltpu.SemaphoreType.DMA((cents // LOAD,)),
             pltpu.SemaphoreType.DMA((groups,)),
             pltpu.SemaphoreType.DMA((groups,)),
             pltpu.SemaphoreType.DMA((9,)),
@@ -432,11 +487,17 @@
             pltpu.SemaphoreType.DMA((len(found.ids),)),
         ],
         compiler_params=pltpu.CompilerParams(
-            collective_id=0, has_side_effects=True, vmem_limit_bytes=58 * 1024 * 1024),
+            collective_id=0, has_side_effects=True, vmem_limit_bytes=56 * 1024 * 1024),
     )(points, centroids)
-    counts = counts.reshape(cents)
-    new_centroids = (sums + prior_mass * centroids.astype(F32)) / (counts + prior_mass)[:, None]
-    return new_centroids, counts, log_evidence.reshape(rows)
+    new_centroids, counts, log_evidence = pl.pallas_call(
+        put_out,
+        out_shape=tuple(jax.ShapeDtypeStruct(r.shape, r.dtype) for r in results),
+        in_specs=[vmem] * 3,
+        out_specs=(pl.BlockSpec(memory_space=pl.ANY),) * 3,
+        scratch_shapes=[pltpu.SemaphoreType.DMA((6,))],
+        compiler_params=pltpu.CompilerParams(vmem_limit_bytes=1024 * 1024),
+    )(*results)
+    return new_centroids, counts.reshape(cents), log_evidence.reshape(rows)
 
 
 def solution(mesh):

time: 81.7 us -> 76.9 us (0.941)
  other arithmetic: 3.59 us -> 0 us
  local copies, waits for them, and re-layouts: 1.2 us -> 0 us
    div x1 -> x0, other arithmetic: 3.58 us -> none  [body(): (sums + prior_mass * centroids.astype(F32)) / (counts + prior_mass)[:, None]]
    pallas_call x0 -> x1, Pallas kernels: none -> 2.07 us  [body(): pl.pallas_call(put_out, out_shape=tuple((jax.ShapeDtypeStruct(r.shape, r....]
    pallas_call x1, Pallas kernels: 75.7 us -> 74 us  [body(): pl.pallas_call(functools.partial(kernel, (rows, cents, width, groups)), o...]
    unnamed x2 -> x0, local copies, waits for them, and re-layouts: 1.2 us -> none
where the time goes in v3:
time: 76.9 us; the launch traced here: 76.8 us
  Pallas kernels  76.1 us (99%)
    pallas_call x1, Pallas kernels, body(): pl.pallas_call(functools.partial(kernel, (rows, cents, width, groups)), o...  74 us
    pallas_call x1, Pallas kernels, body(): pl.pallas_call(put_out, out_shape=tuple((jax.ShapeDtypeStruct(r.shape, r....  2.07 us

profile of v3, /device:TPU:8, one launch (start us, length us, event | category | flops | bytes accessed | tf_op | source)
XLA Modules:
  0.0 76.8 jit_solution(4743220514266392862)
XLA Ops:
  0.6 74.0 %shard_map.49 = (f32[4096,256]{1,0:T(8,128)S(1)}, f32[32,128]{1,0:T(8,128)S(1)}, f32[8,128]{1,0:T(8,128)S(1)}) custom-call(bf16[1024,256]{1,0:T(8,128)(2,1)} %x_ref.1, bf16[4096,256]{1,0:T(8,128)(2,1)} %c_hbm.1), custom_call_target="tpu_custom_call" | custom-call | tf_op jit(solution)/shard_map/pallas_call | solution.py:458
  74.7 2.1 %shard_map.50 = (f32[4096,256]{1,0:T(8,128)}, f32[32,128]{1,0:T(8,128)}, f32[8,128]{1,0:T(8,128)}) custom-call(f32[4096,256]{1,0:T(8,128)S(1)} %get-tuple-element.9.centroids, f32[32,128]{1,0:T(8,128)S(1)} %get-tuple-element.10.counts, f32[8,128]{1,0:T(8,128)S(1)} %get-tuple-element.11.log), custom_call_target="tpu_custom_call" | custom-call | tf_op jit(solution)/shard_map/pallas_call | solution.py:492
